TPU v7x, 32 devices: a whole 2x2x4 slice. The times are simulated.
32 devices in a mesh: groups: 2 (over y), ctx: 4 (over z), dp: 2 (over x), tp: 2 (over core).
Axes of the slice: x: 2, y: 2, z: 4, core: 2. Of those that a mesh axis runs over, the one named last changes fastest.
Arguments:
- queries: bfloat16 [4, 1280, 2048], P(('groups', 'dp'), 'ctx', 'tp'), parts along dimension 0, may hold values from -6 to 6
- key_vectors: bfloat16 [4, 1280, 2048], P(('groups', 'dp'), 'ctx', 'tp'), parts along dimension 0, may hold values from -6 to 6
- value_vectors: bfloat16 [4, 1280, 2048], P(('groups', 'dp'), 'ctx', 'tp'), parts along dimension 0, may hold values from -6 to 6
- grad_output: bfloat16 [4, 1280, 2048], P(('groups', 'dp'), 'ctx', 'tp'), parts along dimension 0, may hold values from -6 to 6
Outputs:
- normed_out: bfloat16 [4, 1280, 2048], P(('groups', 'dp'), 'ctx', 'tp'), parts along dimension 0
- grad_queries: bfloat16 [4, 1280, 2048], P(('groups', 'dp'), 'ctx', 'tp'), parts along dimension 0
- grad_keys: bfloat16 [4, 1280, 2048], P(('groups', 'dp'), 'ctx', 'tp'), parts along dimension 0
- grad_values: bfloat16 [4, 1280, 2048], P(('groups', 'dp'), 'ctx', 'tp'), parts along dimension 0
There are 2 independent parts, one for each index of `groups`. A program takes and returns all parts, laid end to end along the dimension named above; each array names one. Nothing has to cross between parts.
All inputs are finite; a program needn't handle non-finite values.
Results may differ from a plain program's by a relative error of at most 0.0059.
Values may be sent and summed in bfloat16 or wider, within the bound.
No kernel may reach another device: no remote copies, remote signals or barrier semaphores. Data moves between devices by JAX's collectives and lax.ppermute only.
A program may use at most 64 MiB of HBM per device.

v0:
```python
import jax
import jax.numpy as jnp
from jax import lax
from jax.sharding import PartitionSpec as P

DH = 128
norm_eps = 1e-06


def shards(queries, key_vectors, value_vectors, grad_output):
    block_len = queries.shape[1]
    head_count = queries.shape[2] // DH
    query_rows = queries.reshape(block_len, head_count, DH)
    key_rows = key_vectors.reshape(block_len, head_count, DH)
    value_rows = value_vectors.reshape(block_len, head_count, DH)
    grad_rows = grad_output.reshape(block_len, head_count, DH)
    rows = lax.broadcasted_iota(jnp.int32, (block_len, block_len), 0)
    columns = lax.broadcasted_iota(jnp.int32, (block_len, block_len), 1)
    causal = (columns <= rows)[None]
    local_state = jnp.einsum(
        "shd,she->hde", key_rows, value_rows, preferred_element_type=jnp.float32
    )
    state_shape = local_state.shape
    shares = lax.all_to_all(
        local_state.reshape(1, -1), "ctx", split_axis=1, concat_axis=0, tiled=True
    )
    running = jnp.cumsum(shares, axis=0)
    earlier_shares = (running - shares).astype(jnp.bfloat16)
    earlier_low = lax.all_to_all(
        earlier_shares, "ctx", split_axis=0, concat_axis=1, tiled=True
    ).reshape(state_shape)
    raw_scores = jnp.einsum(
        "thd,shd->hts", query_rows, key_rows, preferred_element_type=jnp.float32
    )
    scores_low = jnp.where(causal, raw_scores, 0.0).astype(jnp.bfloat16)
    mixed = jnp.einsum("hts,she->the", scores_low, value_rows, preferred_element_type=jnp.float32)
    mixed = mixed + jnp.einsum(
        "thd,hde->the", query_rows, earlier_low, preferred_element_type=jnp.float32
    )
    inverse = lax.rsqrt(jnp.mean(mixed * mixed, axis=-1, keepdims=True) + norm_eps)
    normed = mixed * inverse
    grad_f = grad_rows.astype(jnp.float32)
    grad_mixed = inverse * (grad_f - normed * jnp.mean(grad_f * normed, axis=-1, keepdims=True))
    grad_low = grad_mixed.astype(jnp.bfloat16)
    grad_state = jnp.einsum(
        "thd,the->hde", query_rows, grad_low, preferred_element_type=jnp.float32
    )
    grad_shares = lax.all_to_all(
        grad_state.reshape(1, -1), "ctx", split_axis=1, concat_axis=0, tiled=True
    )
    grad_total = jnp.sum(grad_shares, axis=0, keepdims=True)
    later_shares = (grad_total - jnp.cumsum(grad_shares, axis=0)).astype(jnp.bfloat16)
    later_low = lax.all_to_all(
        later_shares, "ctx", split_axis=0, concat_axis=1, tiled=True
    ).reshape(state_shape)
    raw_grad = jnp.einsum("the,she->hts", grad_low, value_rows, preferred_element_type=jnp.float32)
    grad_scores = jnp.where(causal, raw_grad, 0.0).astype(jnp.bfloat16)
    grad_q = jnp.einsum("hts,shd->thd", grad_scores, key_rows, preferred_element_type=jnp.float32)
    grad_q = grad_q + jnp.einsum(
        "the,hde->thd", grad_low, earlier_low, preferred_element_type=jnp.float32
    )
    grad_k = jnp.einsum("hts,thd->shd", grad_scores, query_rows, preferred_element_type=jnp.float32)
    grad_k = grad_k + jnp.einsum(
        "she,hde->shd", value_rows, later_low, preferred_element_type=jnp.float32
    )
    grad_v = jnp.einsum("hts,the->she", scores_low, grad_low, preferred_element_type=jnp.float32)
    grad_v = grad_v + jnp.einsum(
        "shd,hde->she", key_rows, later_low, preferred_element_type=jnp.float32
    )
    out_shape = queries.shape
    return (
        normed.astype(jnp.bfloat16).reshape(out_shape),
        grad_q.astype(jnp.bfloat16).reshape(out_shape),
        grad_k.astype(jnp.bfloat16).reshape(out_shape),
        grad_v.astype(jnp.bfloat16).reshape(out_shape),
    )


def solution(mesh):
    placed = (
        P(("groups", "dp"), "ctx", "tp"),
        P(("groups", "dp"), "ctx", "tp"),
        P(("groups", "dp"), "ctx", "tp"),
        P(("groups", "dp"), "ctx", "tp"),
    )
    return jax.shard_map(
        shards,
        mesh=mesh,
        in_specs=placed,
        out_specs=(
            P(("groups", "dp"), "ctx", "tp"),
            P(("groups", "dp"), "ctx", "tp"),
            P(("groups", "dp"), "ctx", "tp"),
            P(("groups", "dp"), "ctx", "tp"),
        ),
        check_vma=False,
    )
```

profile of v0, /device:TPU:0, one launch (start us, length us, event | category | flops | bytes accessed | tf_op | source)
XLA Modules:
  0.0 100.5 jit_solution(13804386962089446467)
XLA Ops:
  0.6 1.3 %copy.92 = bf16[40,8,8,128]{3,2,1,0:T(8,128)(2,1)S(1)} copy(bf16[40,8,8,128]{3,1,2,0:T(8,128)(2,1)} %bitcast.73) | data formatting | bytes 1310720
  2.1 1.2 %fusion.13 = f32[8,128,128]{2,1,0:T(8,128)} fusion(bf16[320,8,128]{2,1,0:T(8,128)(2,1)S(1)} %bitcast.61, bf16[320,8,128]{2,1,0:T(8,128)(2,1)S(1)} %bitcast.65), kind=kOutput, calls=%fused_computation.31 | convolution fusion | flops 83886080 | bytes 1835008 | tf_op jit(solution)/shard_map/shd,she->hde/dot_general | solution.py:20
  3.3 6.3 %all-to-all-start = ((f32[1,4,32768]{2,0,1:T(1,128)}), f32[1,4,32768]{2,0,1:T(1,128)S(1)}, u32[]{:S(2)}, u32[]{:S(2)}) async-start(f32[1,4,32768]{2,0,1:T(1,128)} %bitcast.1), calls=%async_computation | async-start | bytes 1048576 | tf_op jit(solution)/shard_map/all_to_all | solution.py:24
  9.8 2.0 %select_convert_fusion.1 = bf16[8,320,320]{2,1,0:T(8,128)(2,1)} fusion(pred[320,320]{1,0:T(8,128)(4,1)S(1)} %iota_compare_fusion, bf16[320,8,128]{2,1,0:T(8,128)(2,1)S(1)} %bitcast.66, bf16[320,8,128]{2,1,0:T(8,128)(2,1)S(1)} %bitcast.69), kind=kOutput, calls=%fused_computation.5 | convolution fusion | flops 211353600 | bytes 3051520 | tf_op jit(solution)/shard_map/thd,shd->hts/dot_general | solution.py:32
  11.8 12.3 %all-to-all-done = f32[1,4,32768]{2,0,1:T(1,128)S(1)} async-done(((f32[1,4,32768]{2,0,1:T(1,128)}), f32[1,4,32768]{2,0,1:T(1,128)S(1)}, u32[]{:S(2)}, u32[]{:S(2)}) %all-to-all-start) | async-done | bytes 524320 | tf_op jit(solution)/shard_map/all_to_all | solution.py:24
  24.1 0.4 fusion
  24.5 0.5 broadcast.40
  25.0 2.3 %reduce.3 = bf16[4,32768]{1,0:T(4,128)(2,1)S(1)} reduce(bf16[4,1,32768]{2,1,0:T(2,128)(2,1)S(1)} %fusion, bf16[]{:T(256)} %broadcast.40), dimensions={1}, to_apply=%fusion.reduce_sub_computation | reduce | bytes 524290 | tf_op jit(solution)/shard_map/jit(cumsum)/reduce_window_sum | solution.py:27
  27.4 1.0 reshape.148
  28.4 3.4 %all-to-all-start.1 = ((bf16[4,2,16384]{2,1,0:T(2,128)(2,1)}), bf16[4,2,16384]{2,1,0:T(2,128)(2,1)S(1)}, u32[]{:S(2)}, u32[]{:S(2)}) async-start(bf16[4,2,16384]{2,1,0:T(2,128)(2,1)} %reshape.148), calls=%async_computation.1 | async-start | bytes 524288 | tf_op jit(solution)/shard_map/all_to_all | solution.py:29
  31.8 1.2 %convert_bitcast_fusion = f32[40,8,8,128]{3,1,2,0:T(8,128)S(1)} fusion(bf16[1,320,1024]{2,1,0:T(8,128)(2,1)} %param.7), kind=kLoop, calls=%fused_computation.19 | loop fusion | flops 327680 | bytes 1966080
  33.3 1.3 %copy-done.3 = bf16[8,320,320]{2,1,0:T(8,128)(2,1)S(1)} copy-done((bf16[8,320,320]{2,1,0:T(8,128)(2,1)S(1)}, bf16[8,320,320]{2,1,0:T(8,128)(2,1)}, u32[]{:S(2)}) %copy-start.3) | copy-done | bytes 1638424
  34.6 1.7 %convolution_bitcast_fusion.5 = f32[320,8,128]{2,0,1:T(8,128)} fusion(bf16[8,320,320]{2,1,0:T(8,128)(2,1)S(1)} %copy-done.3, bf16[320,8,128]{2,1,0:T(8,128)(2,1)S(1)} %bitcast.62), kind=kOutput, calls=%fused_computation.15 | convolution fusion | flops 209715200 | bytes 3604480 | tf_op jit(solution)/shard_map/hts,she->the/dot_general | solution.py:36
  36.3 3.8 %all-to-all-done.1 = bf16[4,2,16384]{2,1,0:T(2,128)(2,1)S(1)} async-done(((bf16[4,2,16384]{2,1,0:T(2,128)(2,1)}), bf16[4,2,16384]{2,1,0:T(2,128)(2,1)S(1)}, u32[]{:S(2)}, u32[]{:S(2)}) %all-to-all-start.1) | async-done | bytes 262176 | tf_op jit(solution)/shard_map/all_to_all | solution.py:29
  40.1 1.0 reshape.149
  41.1 3.4 %reduce.1 = bf16[4,32768]{1,0:T(4,128)(2,1)} reduce(bf16[4,1,32768]{2,1,0:T(2,128)(2,1)} %reshape.149, bf16[]{:T(256)} %constant.16), dimensions={1}, to_apply=%all_to_all.18.reduce_sub_computation | reduce | bytes 524290 | tf_op jit(solution)/shard_map/all_to_all | solution.py:29
  44.4 1.2 %reshape.139 = bf16[8,128,128]{2,1,0:T(8,128)(2,1)S(1)} reshape(bf16[4,32768]{1,0:T(4,128)(2,1)} %reduce.1) | data formatting | bytes 524288 | tf_op jit(solution)/shard_map/reshape | solution.py:31
  45.7 2.0 %multiply_reduce_fusion.1 = (f32[320,8]{0,1:T(8,128)S(1)}, f32[320,8,128]{2,0,1:T(8,128)S(1)}) fusion(f32[320,8,128]{2,0,1:T(8,128)} %convolution_bitcast_fusion.5, bf16[8,128,128]{2,1,0:T(8,128)(2,1)S(1)} %reshape.139, bf16[320,8,128]{2,1,0:T(8,128)(2,1)S(1)} %bitcast.70), kind=kOutput, calls=%fused_computation.22 | convolution fusion | flops 84866560 | bytes 3549184 | tf_op jit(solution)/shard_map/thd,hde->the/dot_general | solution.py:37
  47.7 0.9 multiply_reduce_fusion
  48.6 1.6 %multiply_convert_fusion = (bf16[320,8,128]{2,0,1:T(8,128)(2,1)S(1)}, bf16[320,8,128]{2,0,1:T(8,128)(2,1)}) fusion(f32[320,8,128]{2,1,0:T(8,128)S(1)} %bitcast.60, f32[320,8,128]{2,0,1:T(8,128)S(1)} %get-tuple-element.7, f32[320,8]{0,1:T(8,128)S(1)} %broadcast_multiply_fusion, f32[320,8]{0,1:T(8,128)S(1)} %add_rsqrt_fusion), kind=kLoop, calls=%fused_computation.20 | loop fusion | flops 1966080 | bytes 3952640 | tf_op jit(solution)/shard_map/convert_element_type | solution.py:44
  50.2 0.4 convolution_bitcast_fusion.6
  50.6 1.0 copy.82
  51.6 4.3 %all-to-all-start.2 = ((f32[1,4,32768]{2,0,1:T(1,128)}), f32[1,4,32768]{2,0,1:T(1,128)}, u32[]{:S(2)}, u32[]{:S(2)}) async-start(f32[1,4,32768]{2,0,1:T(1,128)} %bitcast.8), calls=%async_computation.2 | async-start | bytes 1048576 | tf_op jit(solution)/shard_map/all_to_all | solution.py:48
  56.0 0.7 select_convert_fusion
  56.7 1.3 %copy-done.5 = bf16[8,320,320]{2,1,0:T(8,128)(2,1)} copy-done((bf16[8,320,320]{2,1,0:T(8,128)(2,1)}, bf16[8,320,320]{2,1,0:T(8,128)(2,1)S(1)}, u32[]{:S(2)}) %copy-start.5) | copy-done | bytes 1638424
  57.9 0.7 convolution_bitcast_fusion.4
  58.6 9.6 %all-to-all-done.2 = f32[1,4,32768]{2,0,1:T(1,128)} async-done(((f32[1,4,32768]{2,0,1:T(1,128)}), f32[1,4,32768]{2,0,1:T(1,128)}, u32[]{:S(2)}, u32[]{:S(2)}) %all-to-all-start.2) | async-done | bytes 524320 | tf_op jit(solution)/shard_map/all_to_all | solution.py:48
  68.2 2.2 %reduce_sum.29 = f32[32768]{0:T(1024)} reduce(f32[1,4,32768]{2,0,1:T(1,128)} %all-to-all-done.2, f32[]{:T(128)} %constant.9.clone.1), dimensions={0,1}, to_apply=%region_3.4 | reduce | flops 98304 | bytes 655364 | tf_op jit(solution)/shard_map/reduce_sum | solution.py:51
  70.3 2.3 %fusion.1 = bf16[4,1,32768]{2,1,0:T(2,128)(2,1)} fusion(f32[1,4,32768]{2,0,1:T(1,128)} %all-to-all-done.2, f32[32768]{0:T(1024)} %reduce_sum.29), kind=kOutput, calls=%fused_computation.3 | output fusion | flops 655360 | bytes 917504 | tf_op jit(solution)/shard_map/jit(cumsum)/reduce_window_sum | solution.py:52
  72.6 4.0 %reduce.4 = bf16[4,32768]{1,0:T(4,128)(2,1)} reduce(bf16[4,1,32768]{2,1,0:T(2,128)(2,1)} %fusion.1, bf16[]{:T(256)} %broadcast.40), dimensions={1}, to_apply=%fusion.1.reduce_sub_computation | reduce | bytes 524290 | tf_op jit(solution)/shard_map/jit(cumsum)/reduce_window_sum | solution.py:52
  76.6 2.0 %reshape.150 = bf16[4,2,16384]{2,1,0:T(2,128)(2,1)} reshape(bf16[4,32768]{1,0:T(4,128)(2,1)} %reduce.4) | data formatting | bytes 524288
  78.6 4.0 %all-to-all-start.3 = ((bf16[4,2,16384]{2,1,0:T(2,128)(2,1)}), bf16[4,2,16384]{2,1,0:T(2,128)(2,1)}, u32[]{:S(2)}, u32[]{:S(2)}) async-start(bf16[4,2,16384]{2,1,0:T(2,128)(2,1)} %reshape.150), calls=%async_computation.3 | async-start | bytes 524288 | tf_op jit(solution)/shard_map/all_to_all | solution.py:53
  82.6 1.2 %fusion.5 = bf16[320,8,128]{2,0,1:T(8,128)(2,1)} fusion(f32[320,8,128]{2,0,1:T(8,128)S(1)} %convolution_bitcast_fusion.4, bf16[8,128,128]{2,1,0:T(8,128)(2,1)S(1)} %reshape.139, bf16[320,8,128]{2,0,1:T(8,128)(2,1)S(1)} %get-tuple-element.4), kind=kOutput, calls=%fused_computation.16 | convolution fusion | flops 84541440 | bytes 2883584 | tf_op jit(solution)/shard_map/the,hde->thd/dot_general | solution.py:59
  83.8 0.4 copy.73
  84.3 1.1 %reshape.140 = bf16[1,320,1024]{2,1,0:T(8,128)(2,1)} reshape(bf16[320,8,128]{2,1,0:T(8,128)(2,1)S(1)} %copy.73) | data formatting | bytes 1310720 | tf_op jit(solution)/shard_map/reshape | solution.py:72
  85.4 1.6 %copy.78 = bf16[320,8,128]{2,1,0:T(8,128)(2,1)S(1)} copy(bf16[320,8,128]{2,0,1:T(8,128)(2,1)} %fusion.5) | data formatting | bytes 1310720 | tf_op jit(solution)/shard_map/convert_element_type | solution.py:73
  87.0 1.1 %reshape.141 = bf16[1,320,1024]{2,1,0:T(8,128)(2,1)} reshape(bf16[320,8,128]{2,1,0:T(8,128)(2,1)S(1)} %copy.78) | data formatting | bytes 1310720 | tf_op jit(solution)/shard_map/reshape | solution.py:73
  88.1 3.4 %convolution_bitcast_fusion.2 = f32[320,8,128]{2,0,1:T(8,128)} fusion(bf16[8,320,320]{2,1,0:T(8,128)(2,1)} %copy-done.5, bf16[320,8,128]{2,1,0:T(8,128)(2,1)S(1)} %bitcast.72), kind=kOutput, calls=%fused_computation.11 | convolution fusion | flops 209715200 | bytes 3604480 | tf_op jit(solution)/shard_map/hts,thd->shd/dot_general | solution.py:62
  91.5 1.2 %reshape.151 = bf16[4,1,32768]{2,1,0:T(2,128)(2,1)S(1)} reshape(bf16[4,2,16384]{2,1,0:T(2,128)(2,1)} %all-to-all-done.3) | data formatting | bytes 524288
  92.7 1.7 %reduce.2 = bf16[4,32768]{1,0:T(4,128)(2,1)S(1)} reduce(bf16[4,1,32768]{2,1,0:T(2,128)(2,1)S(1)} %reshape.151, bf16[]{:T(256)} %constant.16), dimensions={1}, to_apply=%all_to_all.41.reduce_sub_computation | reduce | bytes 524290 | tf_op jit(solution)/shard_map/all_to_all | solution.py:53
  94.7 0.3 fusion.16
  95.0 1.2 %copy-done.4 = bf16[8,320,320]{2,1,0:T(8,128)(2,1)S(1)} copy-done((bf16[8,320,320]{2,1,0:T(8,128)(2,1)S(1)}, bf16[8,320,320]{2,1,0:T(8,128)(2,1)}, u32[]{:S(2)}) %copy-start.4) | copy-done | bytes 1638424
  96.2 0.8 fusion.8
  97.1 0.4 copy.88
  97.5 1.1 %reshape.144 = bf16[1,320,1024]{2,1,0:T(8,128)(2,1)} reshape(bf16[320,8,128]{2,1,0:T(8,128)(2,1)S(1)} %copy.88) | data formatting | bytes 1310720 | tf_op jit(solution)/shard_map/reshape | solution.py:75
  98.6 0.3 fusion.6
  99.0 0.4 copy.85
  99.4 1.1 %reshape.143 = bf16[1,320,1024]{2,1,0:T(8,128)(2,1)} reshape(bf16[320,8,128]{2,1,0:T(8,128)(2,1)S(1)} %copy.85) | data formatting | bytes 1310720 | tf_op jit(solution)/shard_map/reshape | solution.py:74
  (29 shorter events, 0.9 us)
Async XLA Ops:
  0.6 1.3 %copy-start.8 = (bf16[1,320,1024]{2,1,0:T(8,128)(2,1)S(1)}, bf16[1,320,1024]{2,1,0:T(8,128)(2,1)}, u32[]{:S(2)}) copy-start(bf16[1,320,1024]{2,1,0:T(8,128)(2,1)} %param.6) | copy-start | bytes 1966084
  2.1 7.6 %copy-start.9 = (bf16[1,320,1024]{2,1,0:T(8,128)(2,1)S(1)}, bf16[1,320,1024]{2,1,0:T(8,128)(2,1)}, u32[]{:S(2)}) copy-start(bf16[1,320,1024]{2,1,0:T(8,128)(2,1)} %param.4) | copy-start | bytes 1966084
  3.3 20.8 %all-to-all-start = ((f32[1,4,32768]{2,0,1:T(1,128)}), f32[1,4,32768]{2,0,1:T(1,128)S(1)}, u32[]{:S(2)}, u32[]{:S(2)}) async-start(f32[1,4,32768]{2,0,1:T(1,128)} %bitcast.1), calls=%async_computation | async-start | bytes 1048576 | tf_op jit(solution)/shard_map/all_to_all | solution.py:24
  9.8 35.9 %copy-start = (bf16[40,8,8,128]{3,2,1,0:T(8,128)(2,1)}, bf16[40,8,8,128]{3,2,1,0:T(8,128)(2,1)S(1)}, u32[]{:S(2)}) copy-start(bf16[40,8,8,128]{3,2,1,0:T(8,128)(2,1)S(1)} %copy.91) | copy-start | bytes 1966084
  9.8 2.0 %copy-start.10 = (pred[320,320]{1,0:T(8,128)(4,1)}, pred[320,320]{1,0:T(8,128)(4,1)S(1)}, u32[]{:S(2)}) copy-start(pred[320,320]{1,0:T(8,128)(4,1)S(1)} %iota_compare_fusion) | copy-start | bytes 307204
  28.4 11.8 %all-to-all-start.1 = ((bf16[4,2,16384]{2,1,0:T(2,128)(2,1)}), bf16[4,2,16384]{2,1,0:T(2,128)(2,1)S(1)}, u32[]{:S(2)}, u32[]{:S(2)}) async-start(bf16[4,2,16384]{2,1,0:T(2,128)(2,1)} %reshape.148), calls=%async_computation.1 | async-start | bytes 524288 | tf_op jit(solution)/shard_map/all_to_all | solution.py:29
  33.0 1.6 %copy-start.3 = (bf16[8,320,320]{2,1,0:T(8,128)(2,1)S(1)}, bf16[8,320,320]{2,1,0:T(8,128)(2,1)}, u32[]{:S(2)}) copy-start(bf16[8,320,320]{2,1,0:T(8,128)(2,1)} %select_convert_fusion.1) | copy-start | bytes 4915204
  48.5 1.6 %copy-start.1 = (bf16[40,8,8,128]{3,2,1,0:T(8,128)(2,1)S(1)}, bf16[40,8,8,128]{3,2,1,0:T(8,128)(2,1)}, u32[]{:S(2)}) copy-start(bf16[40,8,8,128]{3,2,1,0:T(8,128)(2,1)} %copy-done) | copy-start | bytes 1966084
  50.6 5.3 %copy-start.11 = (pred[320,320]{1,0:T(8,128)(4,1)S(1)}, pred[320,320]{1,0:T(8,128)(4,1)}, u32[]{:S(2)}) copy-start(pred[320,320]{1,0:T(8,128)(4,1)} %copy-done.10) | copy-start | bytes 307204
  51.6 16.5 %all-to-all-start.2 = ((f32[1,4,32768]{2,0,1:T(1,128)}), f32[1,4,32768]{2,0,1:T(1,128)}, u32[]{:S(2)}, u32[]{:S(2)}) async-start(f32[1,4,32768]{2,0,1:T(1,128)} %bitcast.8), calls=%async_computation.2 | async-start | bytes 1048576 | tf_op jit(solution)/shard_map/all_to_all | solution.py:48
  56.7 1.3 %copy-start.5 = (bf16[8,320,320]{2,1,0:T(8,128)(2,1)}, bf16[8,320,320]{2,1,0:T(8,128)(2,1)S(1)}, u32[]{:S(2)}) copy-start(bf16[8,320,320]{2,1,0:T(8,128)(2,1)S(1)} %select_convert_fusion) | copy-start | bytes 4915204
  78.6 12.9 %all-to-all-start.3 = ((bf16[4,2,16384]{2,1,0:T(2,128)(2,1)}), bf16[4,2,16384]{2,1,0:T(2,128)(2,1)}, u32[]{:S(2)}, u32[]{:S(2)}) async-start(bf16[4,2,16384]{2,1,0:T(2,128)(2,1)} %reshape.150), calls=%async_computation.3 | async-start | bytes 524288 | tf_op jit(solution)/shard_map/all_to_all | solution.py:53
  82.6 1.2 %copy-start.7 = (bf16[320,8,128]{2,0,1:T(8,128)(2,1)S(1)}, bf16[320,8,128]{2,0,1:T(8,128)(2,1)}, u32[]{:S(2)}) copy-start(bf16[320,8,128]{2,0,1:T(8,128)(2,1)} %get-tuple-element.5) | copy-start | bytes 1966084
  85.4 2.7 %copy-start.2 = (bf16[40,8,8,128]{3,2,1,0:T(8,128)(2,1)S(1)}, bf16[40,8,8,128]{3,2,1,0:T(8,128)(2,1)}, u32[]{:S(2)}) copy-start(bf16[40,8,8,128]{3,2,1,0:T(8,128)(2,1)} %copy-done) | copy-start | bytes 1966084
  94.7 1.5 %copy-start.4 = (bf16[8,320,320]{2,1,0:T(8,128)(2,1)S(1)}, bf16[8,320,320]{2,1,0:T(8,128)(2,1)}, u32[]{:S(2)}) copy-start(bf16[8,320,320]{2,1,0:T(8,128)(2,1)} %select_convert_fusion.1) | copy-start | bytes 4915204
  97.1 1.6 %copy-start.6 = (f32[320,8,128]{2,0,1:T(8,128)S(1)}, f32[320,8,128]{2,0,1:T(8,128)}, u32[]{:S(2)}) copy-start(f32[320,8,128]{2,0,1:T(8,128)} %convolution_bitcast_fusion.2) | copy-start | bytes 3932164
where the time goes:
time: 101 us
  waiting for transfers between devices  25.7 us (25%)
  local copies, waits for them, and re-layouts  21 us (21%)
  other arithmetic  19.9 us (20%)
  starting transfers between devices  18.1 us (18%)
  matrix products  14.8 us (15%)
    all_to_all x1, waiting for transfers between devices, shards(): lax.all_to_all(local_state.reshape(1, -1), 'ctx', split_axis=1, concat_ax...  12.3 us
    unnamed x32, local copies, waits for them, and re-layouts  10.7 us
    all_to_all x1, waiting for transfers between devices, shards(): lax.all_to_all(grad_state.reshape(1, -1), 'ctx', split_axis=1, concat_axi...  9.56 us
    all_to_all x1, starting transfers between devices, shards(): lax.all_to_all(local_state.reshape(1, -1), 'ctx', split_axis=1, concat_ax...  6.32 us
    another operation x2, other arithmetic, shards(): jnp.cumsum(grad_shares, axis=0)  6.27 us
    all_to_all x1, starting transfers between devices, shards(): lax.all_to_all(grad_state.reshape(1, -1), 'ctx', split_axis=1, concat_axi...  4.33 us
    all_to_all x1, starting transfers between devices, shards(): lax.all_to_all(later_shares, 'ctx', split_axis=0, concat_axis=1, tiled=True)  4.04 us
    all_to_all x1, waiting for transfers between devices, shards(): lax.all_to_all(earlier_shares, 'ctx', split_axis=0, concat_axis=1, tiled=...  3.82 us
  transfers between devices with their start and end apart: 4, of which 3 were waited for; matrix products, arithmetic and copies ran while one was open for 15% of the time, Pallas kernels for 0%

commit v1 on v0

--- a/solution.py
+++ b/solution.py
@@ -5,6 +5,28 @@
 
 DH = 128
 norm_eps = 1e-06
+
+
+def cut_along(shard, dim, size):
+    before, after = (shard.shape[:dim], shard.shape[dim + 1 :])
+    return jnp.moveaxis(shard.reshape(*before, size, -1, *after), dim, 0)
+
+
+def in_order(blocks, dim):
+    shape = list(blocks.shape[1:])
+    shape[dim] *= blocks.shape[0]
+    return jnp.moveaxis(blocks, 0, dim).reshape(shape)
+
+
+def swapped_with_each(array, axis, split_dim, concat_dim):
+    size, index = (lax.axis_size(axis), lax.axis_index(axis))
+    pieces = cut_along(array, split_dim, size)
+    gathered = [pieces[index]]
+    for hop in range(1, size):
+        sent = pieces[index ^ hop]
+        gathered.append(lax.ppermute(sent, axis, [(i, i ^ hop) for i in range(size)]))
+    pieces = jnp.stack(gathered)[index ^ jnp.arange(size)]
+    return in_order(pieces, concat_dim)
 
 
 def shards(queries, key_vectors, value_vectors, grad_output):
@@ -21,9 +43,7 @@
         "shd,she->hde", key_rows, value_rows, preferred_element_type=jnp.float32
     )
     state_shape = local_state.shape
-    shares = lax.all_to_all(
-        local_state.reshape(1, -1), "ctx", split_axis=1, concat_axis=0, tiled=True
-    )
+    shares = swapped_with_each(local_state.reshape(1, -1), "ctx", 1, 0)
     running = jnp.cumsum(shares, axis=0)
     earlier_shares = (running - shares).astype(jnp.bfloat16)
     earlier_low = lax.all_to_all(

time: 101 us -> 97.1 us (0.961)
  waiting for transfers between devices: 25.7 us -> 22.4 us
  local copies, waits for them, and re-layouts: 21 us -> 22.5 us
  other arithmetic: 19.9 us -> 18.5 us
    all_to_all x1 -> x0, waiting for transfers between devices: 12.3 us -> none  [shards(): lax.all_to_all(local_state.reshape(1, -1), 'ctx', split_axis=1, concat_ax...]
    ppermute x0 -> x3, waiting for transfers between devices: none -> 8.23 us  [swapped_with_each(): lax.ppermute(sent, axis, [(i, i ^ hop) for i in range(size)])]
    all_to_all x1 -> x0, starting transfers between devices: 6.32 us -> none  [shards(): lax.all_to_all(local_state.reshape(1, -1), 'ctx', split_axis=1, concat_ax...]
    ppermute x0 -> x3, starting transfers between devices: none -> 5.76 us  [swapped_with_each(): lax.ppermute(sent, axis, [(i, i ^ hop) for i in range(size)])]
    another operation x2 -> x1, other arithmetic: 2.72 us -> 0.75 us  [shards(): running = jnp.cumsum(shares, axis=0)]
    convert_element_type x0 -> x2, other arithmetic: none -> 1.1 us  [shards(): earlier_shares = (running - shares).astype(jnp.bfloat16)]
    unnamed x1, other arithmetic: 1.22 us -> 0.14 us
    unnamed x32 -> x34, local copies, waits for them, and re-layouts: 10.7 us -> 10.7 us
  transfers between devices with their start and end apart: 4 -> 6, of which waited for: 3 -> 4; matrix products, arithmetic and copies ran while one was open for 15% -> 15% of each run, Pallas kernels for 0% -> 0%
where the time goes in v1:
time: 97.1 us; the launch traced here: 96.3 us
  local copies, waits for them, and re-layouts  22.5 us (23%)
  waiting for transfers between devices  22.4 us (23%)
  other arithmetic  18.5 us (19%)
  starting transfers between devices  17.9 us (18%)
  matrix products  14 us (14%)
  between operations  1.02 us (1%)
    unnamed x34, local copies, waits for them, and re-layouts  10.7 us
    all_to_all x1, waiting for transfers between devices, shards(): lax.all_to_all(grad_state.reshape(1, -1), 'ctx', split_axis=1, concat_axi...  9.38 us
    ppermute x3, waiting for transfers between devices, swapped_with_each(): lax.ppermute(sent, axis, [(i, i ^ hop) for i in range(size)])  8.23 us
    another operation x2, other arithmetic, shards(): jnp.cumsum(grad_shares, axis=0)  6.27 us
    ppermute x3, starting transfers between devices, swapped_with_each(): lax.ppermute(sent, axis, [(i, i ^ hop) for i in range(size)])  5.76 us
    all_to_all x1, waiting for transfers between devices, shards(): lax.all_to_all(earlier_shares, 'ctx', split_axis=0, concat_axis=1, tiled=...  4.74 us
    all_to_all x1, starting transfers between devices, shards(): lax.all_to_all(grad_state.reshape(1, -1), 'ctx', split_axis=1, concat_axi...  4.33 us
    all_to_all x1, starting transfers between devices, shards(): lax.all_to_all(later_shares, 'ctx', split_axis=0, concat_axis=1, tiled=True)  4.04 us
  transfers between devices with their start and end apart: 6, of which 4 were waited for; matrix products, arithmetic and copies ran while one was open for 15% of the time, Pallas kernels for 0%

profile of v1, /device:TPU:0, one launch (start us, length us, event | category | flops | bytes accessed | tf_op | source)
XLA Modules:
  0.0 96.3 jit_solution(16666794008604194364)
XLA Ops:
  0.7 1.3 %copy.92 = bf16[40,8,8,128]{3,2,1,0:T(8,128)(2,1)S(1)} copy(bf16[40,8,8,128]{3,1,2,0:T(8,128)(2,1)} %bitcast.85) | data formatting | bytes 1310720
  2.1 0.4 fusion.11
  2.8 0.5 constant_dynamic-slice_fusion
  3.2 5.1 %collective-permute-start.2 = (f32[1,32768]{1,0:T(1,128)S(1)}, f32[1,32768]{1,0:T(1,128)S(1)}, u32[]{:S(2)}, u32[]{:S(2)}) collective-permute-start(f32[1,32768]{1,0:T(1,128)S(1)} %get-tuple-element.7), channel_id=1, source_target_pairs={{0,12},{4,8},{8,4},{12,0},{1,13},{5,9},{9,5},{13,1},{2,14},{6,10},... | collective-permute-start | bytes 393224 | tf_op jit(solution)/shard_map/ppermute | solution.py:27
  8.4 0.6 collective-permute-start
  9.2 2.0 %select_convert_fusion.1 = bf16[8,320,320]{2,1,0:T(8,128)(2,1)} fusion(pred[320,320]{1,0:T(8,128)(4,1)S(1)} %iota_compare_fusion, bf16[320,8,128]{2,1,0:T(8,128)(2,1)S(1)} %bitcast.77, bf16[320,8,128]{2,1,0:T(8,128)(2,1)S(1)} %bitcast.80), kind=kOutput, calls=%fused_computation.4 | convolution fusion | flops 211353600 | bytes 3051520 | tf_op jit(solution)/shard_map/thd,shd->hts/dot_general | solution.py:52
  11.2 1.6 %collective-permute-done.2 = f32[1,32768]{1,0:T(1,128)S(1)} collective-permute-done((f32[1,32768]{1,0:T(1,128)S(1)}, f32[1,32768]{1,0:T(1,128)S(1)}, u32[]{:S(2)}, u32[]{:S(2)}) %collective-permute-start.2) | collective-permute-done | bytes 131104 | tf_op jit(solution)/shard_map/ppermute | solution.py:27
  12.8 6.6 %collective-permute-done.1 = f32[1,32768]{1,0:T(1,128)S(1)} collective-permute-done((f32[1,32768]{1,0:T(1,128)S(1)}, f32[1,32768]{1,0:T(1,128)S(1)}, u32[]{:S(2)}, u32[]{:S(2)}) %collective-permute-start.1) | collective-permute-done | bytes 131104 | tf_op jit(solution)/shard_map/ppermute | solution.py:27
  19.4 0.5 maximum_bitcast_fusion
  19.9 0.8 gather_fusion
  20.7 0.7 reduce_window_sum.19
  21.7 0.5 broadcast.75
  22.2 1.0 %reduce.3 = bf16[4,32768]{1,0:T(4,128)(2,1)S(1)} reduce(bf16[4,1,32768]{2,0,1:T(4,128)(2,1)S(1)} %subtract_convert_fusion, bf16[]{:T(256)} %broadcast.75), dimensions={1}, to_apply=%copy.71.reduce_sub_computation | reduce | bytes 524290 | tf_op jit(solution)/shard_map/convert_element_type | solution.py:48
  23.1 1.0 %reshape.163 = bf16[4,2,16384]{2,1,0:T(2,128)(2,1)} reshape(bf16[4,32768]{1,0:T(4,128)(2,1)S(1)} %reduce.3) | data formatting | bytes 524288
  24.1 3.7 %all-to-all-start = ((bf16[4,2,16384]{2,1,0:T(2,128)(2,1)}), bf16[4,2,16384]{2,1,0:T(2,128)(2,1)S(1)}, u32[]{:S(2)}, u32[]{:S(2)}) async-start(bf16[4,2,16384]{2,1,0:T(2,128)(2,1)} %reshape.163), calls=%async_computation | async-start | bytes 524288 | tf_op jit(solution)/shard_map/all_to_all | solution.py:49
  28.3 1.3 %copy-done.3 = bf16[8,320,320]{2,1,0:T(8,128)(2,1)S(1)} copy-done((bf16[8,320,320]{2,1,0:T(8,128)(2,1)S(1)}, bf16[8,320,320]{2,1,0:T(8,128)(2,1)}, u32[]{:S(2)}) %copy-start.3) | copy-done | bytes 1638424
  29.6 1.7 %convolution_bitcast_fusion.5 = f32[320,8,128]{2,0,1:T(8,128)} fusion(bf16[8,320,320]{2,1,0:T(8,128)(2,1)S(1)} %copy-done.3, bf16[320,8,128]{2,1,0:T(8,128)(2,1)S(1)} %bitcast.73), kind=kOutput, calls=%fused_computation.14 | convolution fusion | flops 209715200 | bytes 3604480 | tf_op jit(solution)/shard_map/hts,she->the/dot_general | solution.py:56
  31.3 4.7 %all-to-all-done = bf16[4,2,16384]{2,1,0:T(2,128)(2,1)S(1)} async-done(((bf16[4,2,16384]{2,1,0:T(2,128)(2,1)}), bf16[4,2,16384]{2,1,0:T(2,128)(2,1)S(1)}, u32[]{:S(2)}, u32[]{:S(2)}) %all-to-all-start) | async-done | bytes 262176 | tf_op jit(solution)/shard_map/all_to_all | solution.py:49
  36.1 1.0 reshape.164
  37.0 3.4 %reduce.1 = bf16[4,32768]{1,0:T(4,128)(2,1)} reduce(bf16[4,1,32768]{2,1,0:T(2,128)(2,1)} %reshape.164, bf16[]{:T(256)} %constant.33), dimensions={1}, to_apply=%all_to_all.11.reduce_sub_computation | reduce | bytes 524290 | tf_op jit(solution)/shard_map/all_to_all | solution.py:49
  40.4 1.2 %reshape.144 = bf16[8,128,128]{2,1,0:T(8,128)(2,1)S(1)} reshape(bf16[4,32768]{1,0:T(4,128)(2,1)} %reduce.1) | data formatting | bytes 524288 | tf_op jit(solution)/shard_map/reshape | solution.py:51
  41.6 2.0 %multiply_reduce_fusion.1 = (f32[320,8]{0,1:T(8,128)S(1)}, f32[320,8,128]{2,0,1:T(8,128)S(1)}) fusion(f32[320,8,128]{2,0,1:T(8,128)} %convolution_bitcast_fusion.5, bf16[8,128,128]{2,1,0:T(8,128)(2,1)S(1)} %reshape.144, bf16[320,8,128]{2,1,0:T(8,128)(2,1)S(1)} %bitcast.81), kind=kOutput, calls=%fused_computation.21 | convolution fusion | flops 84866560 | bytes 3549184 | tf_op jit(solution)/shard_map/thd,hde->the/dot_general | solution.py:57
  43.6 0.9 multiply_reduce_fusion
  44.5 1.6 %multiply_convert_fusion = (bf16[320,8,128]{2,0,1:T(8,128)(2,1)S(1)}, bf16[320,8,128]{2,0,1:T(8,128)(2,1)}) fusion(f32[320,8,128]{2,1,0:T(8,128)S(1)} %bitcast.71, f32[320,8,128]{2,0,1:T(8,128)S(1)} %get-tuple-element.11, f32[320,8]{0,1:T(8,128)S(1)} %broadcast_multiply_fusion, f32[320,8]{0,1:T(8,128)S(1)} %add_rsqrt_fusion), kind=kLoop, calls=%fused_computation.19 | loop fusion | flops 1966080 | bytes 3952640 | tf_op jit(solution)/shard_map/convert_element_type | solution.py:64
  46.1 0.4 convolution_bitcast_fusion.6
  46.6 1.0 %copy.82 = f32[8,128,128]{2,1,0:T(8,128)} copy(f32[8,128,128]{1,2,0:T(8,128)S(1)} %convolution_bitcast_fusion.6) | data formatting | bytes 1048576 | tf_op jit(solution)/shard_map/thd,the->hde/dot_general | solution.py:65
  47.6 4.3 %all-to-all-start.1 = ((f32[1,4,32768]{2,0,1:T(1,128)}), f32[1,4,32768]{2,0,1:T(1,128)}, u32[]{:S(2)}, u32[]{:S(2)}) async-start(f32[1,4,32768]{2,0,1:T(1,128)} %bitcast.15), calls=%async_computation.1 | async-start | bytes 1048576 | tf_op jit(solution)/shard_map/all_to_all | solution.py:68
  51.9 0.7 select_convert_fusion
  52.6 1.3 %copy-done.5 = bf16[8,320,320]{2,1,0:T(8,128)(2,1)} copy-done((bf16[8,320,320]{2,1,0:T(8,128)(2,1)}, bf16[8,320,320]{2,1,0:T(8,128)(2,1)S(1)}, u32[]{:S(2)}) %copy-start.5) | copy-done | bytes 1638424
  53.9 0.7 convolution_bitcast_fusion.4
  54.6 9.4 %all-to-all-done.1 = f32[1,4,32768]{2,0,1:T(1,128)} async-done(((f32[1,4,32768]{2,0,1:T(1,128)}), f32[1,4,32768]{2,0,1:T(1,128)}, u32[]{:S(2)}, u32[]{:S(2)}) %all-to-all-start.1) | async-done | bytes 524320 | tf_op jit(solution)/shard_map/all_to_all | solution.py:68
  64.0 2.2 %reduce_sum.29 = f32[32768]{0:T(1024)} reduce(f32[1,4,32768]{2,0,1:T(1,128)} %all-to-all-done.1, f32[]{:T(128)} %constant.10.clone.1), dimensions={0,1}, to_apply=%region_3.4 | reduce | flops 98304 | bytes 655364 | tf_op jit(solution)/shard_map/reduce_sum | solution.py:71
  66.1 2.3 %fusion = bf16[4,1,32768]{2,1,0:T(2,128)(2,1)} fusion(f32[1,4,32768]{2,0,1:T(1,128)} %all-to-all-done.1, f32[32768]{0:T(1024)} %reduce_sum.29), kind=kOutput, calls=%fused_computation.2 | output fusion | flops 655360 | bytes 917504 | tf_op jit(solution)/shard_map/jit(cumsum)/reduce_window_sum | solution.py:72
  68.4 4.0 %reduce.4 = bf16[4,32768]{1,0:T(4,128)(2,1)} reduce(bf16[4,1,32768]{2,1,0:T(2,128)(2,1)} %fusion, bf16[]{:T(256)} %broadcast.75), dimensions={1}, to_apply=%fusion.reduce_sub_computation | reduce | bytes 524290 | tf_op jit(solution)/shard_map/jit(cumsum)/reduce_window_sum | solution.py:72
  72.4 2.0 %reshape.165 = bf16[4,2,16384]{2,1,0:T(2,128)(2,1)} reshape(bf16[4,32768]{1,0:T(4,128)(2,1)} %reduce.4) | data formatting | bytes 524288
  74.4 4.0 %all-to-all-start.2 = ((bf16[4,2,16384]{2,1,0:T(2,128)(2,1)}), bf16[4,2,16384]{2,1,0:T(2,128)(2,1)}, u32[]{:S(2)}, u32[]{:S(2)}) async-start(bf16[4,2,16384]{2,1,0:T(2,128)(2,1)} %reshape.165), calls=%async_computation.2 | async-start | bytes 524288 | tf_op jit(solution)/shard_map/all_to_all | solution.py:73
  78.4 1.2 %fusion.4 = bf16[320,8,128]{2,0,1:T(8,128)(2,1)} fusion(f32[320,8,128]{2,0,1:T(8,128)S(1)} %convolution_bitcast_fusion.4, bf16[8,128,128]{2,1,0:T(8,128)(2,1)S(1)} %reshape.144, bf16[320,8,128]{2,0,1:T(8,128)(2,1)S(1)} %get-tuple-element.4), kind=kOutput, calls=%fused_computation.15 | convolution fusion | flops 84541440 | bytes 2883584 | tf_op jit(solution)/shard_map/the,hde->thd/dot_general | solution.py:79
  80.0 1.1 %reshape.145 = bf16[1,320,1024]{2,1,0:T(8,128)(2,1)} reshape(bf16[320,8,128]{2,1,0:T(8,128)(2,1)S(1)} %copy.73) | data formatting | bytes 1310720 | tf_op jit(solution)/shard_map/reshape | solution.py:92
  81.2 1.6 %copy.78 = bf16[320,8,128]{2,1,0:T(8,128)(2,1)S(1)} copy(bf16[320,8,128]{2,0,1:T(8,128)(2,1)} %fusion.4) | data formatting | bytes 1310720 | tf_op jit(solution)/shard_map/convert_element_type | solution.py:93
  82.7 1.1 %reshape.146 = bf16[1,320,1024]{2,1,0:T(8,128)(2,1)} reshape(bf16[320,8,128]{2,1,0:T(8,128)(2,1)S(1)} %copy.78) | data formatting | bytes 1310720 | tf_op jit(solution)/shard_map/reshape | solution.py:93
  83.9 3.4 %convolution_bitcast_fusion.2 = f32[320,8,128]{2,0,1:T(8,128)} fusion(bf16[8,320,320]{2,1,0:T(8,128)(2,1)} %copy-done.5, bf16[320,8,128]{2,1,0:T(8,128)(2,1)S(1)} %bitcast.83), kind=kOutput, calls=%fused_computation.10 | convolution fusion | flops 209715200 | bytes 3604480 | tf_op jit(solution)/shard_map/hts,thd->shd/dot_general | solution.py:82
  87.3 1.2 %reshape.166 = bf16[4,1,32768]{2,1,0:T(2,128)(2,1)S(1)} reshape(bf16[4,2,16384]{2,1,0:T(2,128)(2,1)} %all-to-all-done.2) | data formatting | bytes 524288
  88.5 1.7 %reduce.2 = bf16[4,32768]{1,0:T(4,128)(2,1)S(1)} reduce(bf16[4,1,32768]{2,1,0:T(2,128)(2,1)S(1)} %reshape.166, bf16[]{:T(256)} %constant.33), dimensions={1}, to_apply=%all_to_all.14.reduce_sub_computation | reduce | bytes 524290 | tf_op jit(solution)/shard_map/all_to_all | solution.py:73
  90.8 1.2 %copy-done.4 = bf16[8,320,320]{2,1,0:T(8,128)(2,1)S(1)} copy-done((bf16[8,320,320]{2,1,0:T(8,128)(2,1)S(1)}, bf16[8,320,320]{2,1,0:T(8,128)(2,1)}, u32[]{:S(2)}) %copy-start.4) | copy-done | bytes 1638424
  92.0 0.8 fusion.7
  92.8 0.4 copy.88
  93.3 1.1 %reshape.149 = bf16[1,320,1024]{2,1,0:T(8,128)(2,1)} reshape(bf16[320,8,128]{2,1,0:T(8,128)(2,1)S(1)} %copy.88) | data formatting | bytes 1310720 | tf_op jit(solution)/shard_map/reshape | solution.py:95
  95.2 1.1 %reshape.148 = bf16[1,320,1024]{2,1,0:T(8,128)(2,1)} reshape(bf16[320,8,128]{2,1,0:T(8,128)(2,1)S(1)} %copy.85) | data formatting | bytes 1310720 | tf_op jit(solution)/shard_map/reshape | solution.py:94
  (42 shorter events, 2.9 us)
Async XLA Ops:
  0.6 1.3 %copy-start.8 = (bf16[1,320,1024]{2,1,0:T(8,128)(2,1)S(1)}, bf16[1,320,1024]{2,1,0:T(8,128)(2,1)}, u32[]{:S(2)}) copy-start(bf16[1,320,1024]{2,1,0:T(8,128)(2,1)} %param.6) | copy-start | bytes 1966084
  2.5 6.5 %copy-start.9 = (bf16[1,320,1024]{2,1,0:T(8,128)(2,1)S(1)}, bf16[1,320,1024]{2,1,0:T(8,128)(2,1)}, u32[]{:S(2)}) copy-start(bf16[1,320,1024]{2,1,0:T(8,128)(2,1)} %param.4) | copy-start | bytes 1966084
  3.2 9.5 %collective-permute-start.2 = (f32[1,32768]{1,0:T(1,128)S(1)}, f32[1,32768]{1,0:T(1,128)S(1)}, u32[]{:S(2)}, u32[]{:S(2)}) collective-permute-start(f32[1,32768]{1,0:T(1,128)S(1)} %get-tuple-element.7), channel_id=1, source_target_pairs={{0,12},{4,8},{8,4},{12,0},{1,13},{5,9},{9,5},{13,1},{2,14},{6,10},... | collective-permute-start | bytes 393224 | tf_op jit(solution)/shard_map/ppermute | solution.py:27
  8.3 11.1 %collective-permute-start.1 = (f32[1,32768]{1,0:T(1,128)S(1)}, f32[1,32768]{1,0:T(1,128)S(1)}, u32[]{:S(2)}, u32[]{:S(2)}) collective-permute-start(f32[1,32768]{1,0:T(1,128)S(1)} %get-tuple-element.8), channel_id=1, source_target_pairs={{0,8},{4,12},{8,0},{12,4},{1,9},{5,13},{9,1},{13,5},{2,10},{6,14},... | collective-permute-start | bytes 393224 | tf_op jit(solution)/shard_map/ppermute | solution.py:27
  8.4 11.1 %collective-permute-start = (f32[1,32768]{1,0:T(1,128)S(1)}, f32[1,32768]{1,0:T(1,128)S(1)}, u32[]{:S(2)}, u32[]{:S(2)}) collective-permute-start(f32[1,32768]{1,0:T(1,128)S(1)} %get-tuple-element.9), channel_id=1, source_target_pairs={{0,4},{4,0},{8,12},{12,8},{1,5},{5,1},{9,13},{13,9},{2,6},{6,2},{1... | collective-permute-start | bytes 393224 | tf_op jit(solution)/shard_map/ppermute | solution.py:27
  9.0 2.1 %copy-start.11 = (pred[320,320]{1,0:T(8,128)(4,1)}, pred[320,320]{1,0:T(8,128)(4,1)S(1)}, u32[]{:S(2)}) copy-start(pred[320,320]{1,0:T(8,128)(4,1)S(1)} %iota_compare_fusion) | copy-start | bytes 307204
  9.2 32.5 %copy-start = (bf16[40,8,8,128]{3,2,1,0:T(8,128)(2,1)}, bf16[40,8,8,128]{3,2,1,0:T(8,128)(2,1)S(1)}, u32[]{:S(2)}) copy-start(bf16[40,8,8,128]{3,2,1,0:T(8,128)(2,1)S(1)} %copy.91) | copy-start | bytes 1966084
  21.6 6.3 %copy-start.10 = (bf16[1,320,1024]{2,1,0:T(8,128)(2,1)S(1)}, bf16[1,320,1024]{2,1,0:T(8,128)(2,1)}, u32[]{:S(2)}) copy-start(bf16[1,320,1024]{2,1,0:T(8,128)(2,1)} %param.7) | copy-start | bytes 1966084
  24.1 11.9 %all-to-all-start = ((bf16[4,2,16384]{2,1,0:T(2,128)(2,1)}), bf16[4,2,16384]{2,1,0:T(2,128)(2,1)S(1)}, u32[]{:S(2)}, u32[]{:S(2)}) async-start(bf16[4,2,16384]{2,1,0:T(2,128)(2,1)} %reshape.163), calls=%async_computation | async-start | bytes 524288 | tf_op jit(solution)/shard_map/all_to_all | solution.py:49
  28.0 1.6 %copy-start.3 = (bf16[8,320,320]{2,1,0:T(8,128)(2,1)S(1)}, bf16[8,320,320]{2,1,0:T(8,128)(2,1)}, u32[]{:S(2)}) copy-start(bf16[8,320,320]{2,1,0:T(8,128)(2,1)} %select_convert_fusion.1) | copy-start | bytes 4915204
  44.5 1.6 %copy-start.1 = (bf16[40,8,8,128]{3,2,1,0:T(8,128)(2,1)S(1)}, bf16[40,8,8,128]{3,2,1,0:T(8,128)(2,1)}, u32[]{:S(2)}) copy-start(bf16[40,8,8,128]{3,2,1,0:T(8,128)(2,1)} %copy-done) | copy-start | bytes 1966084
  46.6 5.3 %copy-start.12 = (pred[320,320]{1,0:T(8,128)(4,1)S(1)}, pred[320,320]{1,0:T(8,128)(4,1)}, u32[]{:S(2)}) copy-start(pred[320,320]{1,0:T(8,128)(4,1)} %copy-done.11) | copy-start | bytes 307204
  47.6 16.4 %all-to-all-start.1 = ((f32[1,4,32768]{2,0,1:T(1,128)}), f32[1,4,32768]{2,0,1:T(1,128)}, u32[]{:S(2)}, u32[]{:S(2)}) async-start(f32[1,4,32768]{2,0,1:T(1,128)} %bitcast.15), calls=%async_computation.1 | async-start | bytes 1048576 | tf_op jit(solution)/shard_map/all_to_all | solution.py:68
  52.6 1.3 %copy-start.5 = (bf16[8,320,320]{2,1,0:T(8,128)(2,1)}, bf16[8,320,320]{2,1,0:T(8,128)(2,1)S(1)}, u32[]{:S(2)}) copy-start(bf16[8,320,320]{2,1,0:T(8,128)(2,1)S(1)} %select_convert_fusion) | copy-start | bytes 4915204
  74.4 12.9 %all-to-all-start.2 = ((bf16[4,2,16384]{2,1,0:T(2,128)(2,1)}), bf16[4,2,16384]{2,1,0:T(2,128)(2,1)}, u32[]{:S(2)}, u32[]{:S(2)}) async-start(bf16[4,2,16384]{2,1,0:T(2,128)(2,1)} %reshape.165), calls=%async_computation.2 | async-start | bytes 524288 | tf_op jit(solution)/shard_map/all_to_all | solution.py:73
  78.4 1.2 %copy-start.7 = (bf16[320,8,128]{2,0,1:T(8,128)(2,1)S(1)}, bf16[320,8,128]{2,0,1:T(8,128)(2,1)}, u32[]{:S(2)}) copy-start(bf16[320,8,128]{2,0,1:T(8,128)(2,1)} %get-tuple-element.5) | copy-start | bytes 1966084
  81.2 2.7 %copy-start.2 = (bf16[40,8,8,128]{3,2,1,0:T(8,128)(2,1)S(1)}, bf16[40,8,8,128]{3,2,1,0:T(8,128)(2,1)}, u32[]{:S(2)}) copy-start(bf16[40,8,8,128]{3,2,1,0:T(8,128)(2,1)} %copy-done) | copy-start | bytes 1966084
  90.4 1.5 %copy-start.4 = (bf16[8,320,320]{2,1,0:T(8,128)(2,1)S(1)}, bf16[8,320,320]{2,1,0:T(8,128)(2,1)}, u32[]{:S(2)}) copy-start(bf16[8,320,320]{2,1,0:T(8,128)(2,1)} %select_convert_fusion.1) | copy-start | bytes 4915204
  92.8 1.6 %copy-start.6 = (f32[320,8,128]{2,0,1:T(8,128)S(1)}, f32[320,8,128]{2,0,1:T(8,128)}, u32[]{:S(2)}) copy-start(f32[320,8,128]{2,0,1:T(8,128)} %convolution_bitcast_fusion.2) | copy-start | bytes 3932164
